TPU v7x, 512 devices: a whole 4x4x16 slice. The times are simulated.
512 devices in a mesh: blk: 128 (over y_hi, x, z), feat: 4 (over y_lo, core).
Axes of the slice: x: 4, y: 4 (y_hi: 2, y_lo: 2; y = y_hi * 2 + y_lo), z: 16, core: 2. Of those that a mesh axis runs over, the one named last changes fastest.
Arguments:
- points: bfloat16 [16384, 8192], P('blk', 'feat'), may hold values from -12 to 12
- centers: bfloat16 [2048, 8192], P('blk', 'feat'), may hold values from -12 to 12
- coefs: bfloat16 [2048, 1024], P('blk', 'feat'), may hold values from -16 to 16
Outputs:
- normal_prod: float32 [2048, 1024], P('blk', 'feat')
All inputs are finite; a program needn't handle non-finite values.
Results may differ from a plain program's by a relative error of at most 0.0011.
Values may be sent and summed in bfloat16 or wider, within the bound.
A program may use at most 64 MiB of HBM per device.

v0:
```python
import math
import jax
import jax.numpy as jnp
from jax import lax
from jax.sharding import PartitionSpec as P

F = 8192


def on_device(points, centers, coefs):
    point_sq = jnp.einsum("nf,nf->n", points, points, preferred_element_type=jnp.float32)
    center_piece = lax.all_gather(centers, "blk", axis=0, tiled=True)
    center_sq = jnp.einsum(
        "mf,mf->m", center_piece, center_piece, preferred_element_type=jnp.float32
    )
    cross_dot = lax.dot_general(
        points, center_piece, (((1,), (1,)), ((), ())), preferred_element_type=jnp.float32
    )
    dist_tile = point_sq[:, None] + center_sq[None, :] - 2.0 * cross_dot
    all_coefs = lax.all_gather(coefs, "blk", axis=0, tiled=True)
    dist = lax.psum(dist_tile, "feat")
    kernel = jnp.exp(-dist / F).astype(jnp.bfloat16)
    fitted = jnp.dot(kernel, all_coefs, preferred_element_type=jnp.float32).astype(jnp.bfloat16)
    summed = lax.psum_scatter(
        lax.dot_general(
            kernel, fitted, (((0,), (0,)), ((), ())), preferred_element_type=jnp.float32
        ),
        "blk",
        scatter_dimension=0,
        tiled=True,
    )
    point_total = points.shape[0] * lax.axis_size("blk")
    return summed * (1.0 / math.sqrt(point_total))


def solution(mesh):
    in_specs = (P("blk", "feat"), P("blk", "feat"), P("blk", "feat"))
    out_specs = P("blk", "feat")
    return jax.shard_map(
        on_device, mesh=mesh, in_specs=in_specs, out_specs=out_specs, check_vma=False
    )
```

profile of v0, /device:TPU:8, one launch (start us, length us, event | category | flops | bytes accessed | tf_op | source)
XLA Modules:
  0.0 1248.8 jit_solution(10905283807911872829)
XLA Ops:
  6.5 0.0 copy-start.1
  6.5 0.0 all-gather.3.cloned.1.call-start
  6.5 0.7 all-gather.3.cloned.1.call-update
  7.3 0.0 all-gather.5.cloned.1.call-start
  7.3 0.7 all-gather.5.cloned.1.call-update
  8.0 0.0 all-reduce.2.cloned.1.call-start
  8.1 1.2 fusion.3
  9.3 246.9 %all-gather.3.cloned.1.call-done = bf16[2048,2048]{1,0:T(8,128)(2,1)} async-done(((bf16[16,2048]{1,0:T(8,128)(2,1)}), bf16[2048,2048]{1,0:T(8,128)(2,1)}) %all-gather.3.cloned.1.call-update) | async-done | bytes 8388624 | tf_op jit(solution)/shard_map/all_gather | solution.py:12
  256.2 0.0 copy-start
  256.2 5.2 fusion
  261.5 0.0 copy-done.1
  261.5 0.5 copy-done
  262.0 3.9 fusion.1
  265.9 0.0 all-reduce.2.cloned.1.call-update
  265.9 0.0 reduce-scatter.2.cloned.1.call-start
  266.0 184.1 %all-gather.5.cloned.1.call-done = bf16[2048,256]{1,0:T(8,128)(2,1)} async-done(((bf16[16,256]{1,0:T(8,128)(2,1)}), bf16[2048,256]{1,0:T(8,128)(2,1)}) %all-gather.5.cloned.1.call-update) | async-done | bytes 1048592 | tf_op jit(solution)/shard_map/all_gather | solution.py:20
  450.1 54.6 %all-reduce.2.cloned.1.call-done = f32[128,2048]{1,0:T(8,128)} async-done(((f32[128,2048]{1,0:T(8,128)}), f32[128,2048]{1,0:T(8,128)}) %all-reduce.2.cloned.1.call-update) | async-done | bytes 1048592 | tf_op jit(solution)/shard_map/psum | solution.py:21
  504.7 4.2 fusion.2
  508.9 0.0 reduce-scatter.2.cloned.1.call-update
  508.9 732.0 %reduce-scatter.2.cloned.1.call-done = f32[16,256]{1,0:T(8,128)} async-done(((f32[2048,256]{1,0:T(8,128)}), f32[16,256]{1,0:T(8,128)}) %reduce-scatter.2.cloned.1.call-update) | async-done | bytes 16400 | tf_op jit(solution)/shard_map/reduce_scatter | solution.py:24
  1241.0 1.3 broadcast_multiply_fusion
Async XLA Ops:
  6.5 254.9 %copy-start.1 = (bf16[128,2048]{1,0:T(8,128)(2,1)S(1)}, bf16[128,2048]{1,0:T(8,128)(2,1)}, u32[]{:S(2)}) copy-start(bf16[128,2048]{1,0:T(8,128)(2,1)} %param.3) | copy-start | bytes 1572868
  6.5 249.7 %all-gather.3.cloned.1.call-start = ((), (), s32[]{:S(2)}) async-start(), calls=%async_computation.1 | async-start | bytes 8454144 | tf_op jit(solution)/shard_map/all_gather | solution.py:12
  7.3 442.8 %all-gather.5.cloned.1.call-start = ((), (), s32[]{:S(2)}) async-start(), calls=%async_computation.3 | async-start | bytes 1056768 | tf_op jit(solution)/shard_map/all_gather | solution.py:20
  8.0 496.7 %all-reduce.2.cloned.1.call-start = ((), (), s32[]{:S(2)}) async-start(), calls=%async_computation.2 | async-start | bytes 2097152 | tf_op jit(solution)/shard_map/psum | solution.py:21
  256.2 5.8 copy-start
  265.9 975.0 %reduce-scatter.2.cloned.1.call-start = ((), (), s32[]{:S(2)}) async-start(), calls=%async_computation.4 | async-start | bytes 2113536 | tf_op jit(solution)/shard_map/reduce_scatter | solution.py:24
Sparse Core Ops, SparseCore 0:
  11.8 244.3 all-gather.2
  260.5 189.5 all-gather.4
  453.1 51.5 all-reduce.1
  509.0 731.8 reduce-scatter.1
where the time goes:
time: 1250 us
  waiting for transfers between devices  1220 us (98%)
  between operations  13.1 us (1%)
    reduce_scatter x1, waiting for transfers between devices, on_device(): lax.psum_scatter(lax.dot_general(kernel, fitted, (((0,), (0,)), ((), ()))...  732 us
    all_gather x1, waiting for transfers between devices, on_device(): center_piece = lax.all_gather(centers, 'blk', axis=0, tiled=True)  247 us
    all_gather x1, waiting for transfers between devices, on_device(): all_coefs = lax.all_gather(coefs, 'blk', axis=0, tiled=True)  184 us
    psum x1, waiting for transfers between devices, on_device(): dist = lax.psum(dist_tile, 'feat')  54.6 us
  transfers between devices with their start and end apart: 4, of which 4 were waited for; matrix products, arithmetic and copies ran while one was open for 1% of the time, Pallas kernels for 0%

commit v1 on v0

--- a/solution.py
+++ b/solution.py
@@ -17,7 +17,9 @@
         points, center_piece, (((1,), (1,)), ((), ())), preferred_element_type=jnp.float32
     )
     dist_tile = point_sq[:, None] + center_sq[None, :] - 2.0 * cross_dot
-    all_coefs = lax.all_gather(coefs, "blk", axis=0, tiled=True)
+    all_coefs = jnp.concatenate(
+        lax.all_to_all(jnp.stack([coefs] * lax.axis_size("blk")), "blk", 0, 0), axis=0
+    )
     dist = lax.psum(dist_tile, "feat")
     kernel = jnp.exp(-dist / F).astype(jnp.bfloat16)
     fitted = jnp.dot(kernel, all_coefs, preferred_element_type=jnp.float32).astype(jnp.bfloat16)

time: 1250 us -> 1070 us (0.86)
  waiting for transfers between devices: 1220 us -> 1010 us
  starting transfers between devices: 0.12 us -> 21.6 us
    all_gather x1 -> x0, waiting for transfers between devices: 184 us -> none  [on_device(): all_coefs = lax.all_gather(coefs, 'blk', axis=0, tiled=True)]
    all_to_all x0 -> x1, starting transfers between devices: none -> 21.5 us  [on_device(): lax.all_to_all(jnp.stack([coefs] * lax.axis_size('blk')), 'blk', 0, 0)]
    all_gather x1, waiting for transfers between devices: 247 us -> 228 us  [on_device(): center_piece = lax.all_gather(centers, 'blk', axis=0, tiled=True)]
  transfers between devices with their start and end apart: 4 -> 4, of which waited for: 4 -> 3; matrix products, arithmetic and copies ran while one was open for 1% -> 1% of each run, Pallas kernels for 0% -> 0%
where the time goes in v1:
time: 1070 us
  waiting for transfers between devices  1010 us (94%)
  starting transfers between devices  21.6 us (2%)
  between operations  13.1 us (1%)
    reduce_scatter x1, waiting for transfers between devices, on_device(): lax.psum_scatter(lax.dot_general(kernel, fitted, (((0,), (0,)), ((), ()))...  732 us
    all_gather x1, waiting for transfers between devices, on_device(): center_piece = lax.all_gather(centers, 'blk', axis=0, tiled=True)  228 us
    psum x1, waiting for transfers between devices, on_device(): dist = lax.psum(dist_tile, 'feat')  51.8 us
    all_to_all x1, starting transfers between devices, on_device(): lax.all_to_all(jnp.stack([coefs] * lax.axis_size('blk')), 'blk', 0, 0)  21.5 us
  transfers between devices with their start and end apart: 4, of which 3 were waited for; matrix products, arithmetic and copies ran while one was open for 1% of the time, Pallas kernels for 0%

profile of v1, /device:TPU:8, one launch (start us, length us, event | category | flops | bytes accessed | tf_op | source)
XLA Modules:
  0.0 1065.2 jit_solution(4306252619298720124)
XLA Ops:
  6.5 0.0 copy-start.1
  6.5 0.0 all-gather.2.cloned.1.call-start
  6.5 0.7 all-gather.2.cloned.1.call-update
  7.3 1.8 stack.2
  9.1 21.5 %all-to-all-start = ((bf16[128,16,256]{2,1,0:T(8,128)(2,1)}), bf16[128,16,256]{2,1,0:T(8,128)(2,1)S(1)}, u32[]{:S(2)}, u32[]{:S(2)}) async-start(bf16[128,16,256]{2,1,0:T(8,128)(2,1)} %stack.2), calls=%async_computation | async-start | bytes 2097152 | tf_op jit(solution)/shard_map/all_to_all | solution.py:21
  30.6 0.0 all-reduce.2.cloned.1.call-start
  30.6 1.2 fusion.3
  31.9 227.9 %all-gather.2.cloned.1.call-done = bf16[2048,2048]{1,0:T(8,128)(2,1)} async-done(((bf16[16,2048]{1,0:T(8,128)(2,1)}), bf16[2048,2048]{1,0:T(8,128)(2,1)}) %all-gather.2.cloned.1.call-update) | async-done | bytes 8388624 | tf_op jit(solution)/shard_map/all_gather | solution.py:12
  259.8 0.0 copy-start
  259.8 5.2 fusion
  265.0 0.0 copy-done.1
  265.0 0.5 copy-done
  265.5 3.9 fusion.1
  269.4 0.0 all-reduce.2.cloned.1.call-update
  269.5 0.0 reduce-scatter.2.cloned.1.call-start
  269.5 0.0 all-to-all-done
  269.5 51.8 %all-reduce.2.cloned.1.call-done = f32[128,2048]{1,0:T(8,128)} async-done(((f32[128,2048]{1,0:T(8,128)}), f32[128,2048]{1,0:T(8,128)}) %all-reduce.2.cloned.1.call-update) | async-done | bytes 1048592 | tf_op jit(solution)/shard_map/psum | solution.py:23
  321.3 3.9 fusion.2
  325.3 0.0 reduce-scatter.2.cloned.1.call-update
  325.3 732.0 %reduce-scatter.2.cloned.1.call-done = f32[16,256]{1,0:T(8,128)} async-done(((f32[2048,256]{1,0:T(8,128)}), f32[16,256]{1,0:T(8,128)}) %reduce-scatter.2.cloned.1.call-update) | async-done | bytes 16400 | tf_op jit(solution)/shard_map/reduce_scatter | solution.py:26
  1057.3 1.3 broadcast_multiply_fusion
Async XLA Ops:
  6.5 258.5 %copy-start.1 = (bf16[128,2048]{1,0:T(8,128)(2,1)S(1)}, bf16[128,2048]{1,0:T(8,128)(2,1)}, u32[]{:S(2)}) copy-start(bf16[128,2048]{1,0:T(8,128)(2,1)} %param.3) | copy-start | bytes 1572868
  6.5 253.2 %all-gather.2.cloned.1.call-start = ((), (), s32[]{:S(2)}) async-start(), calls=%async_computation.2 | async-start | bytes 8454144 | tf_op jit(solution)/shard_map/all_gather | solution.py:12
  9.1 260.4 %all-to-all-start = ((bf16[128,16,256]{2,1,0:T(8,128)(2,1)}), bf16[128,16,256]{2,1,0:T(8,128)(2,1)S(1)}, u32[]{:S(2)}, u32[]{:S(2)}) async-start(bf16[128,16,256]{2,1,0:T(8,128)(2,1)} %stack.2), calls=%async_computation | async-start | bytes 2097152 | tf_op jit(solution)/shard_map/all_to_all | solution.py:21
  30.6 290.8 %all-reduce.2.cloned.1.call-start = ((), (), s32[]{:S(2)}) async-start(), calls=%async_computation.3 | async-start | bytes 2097152 | tf_op jit(solution)/shard_map/psum | solution.py:23
  259.8 5.8 copy-start
  269.5 787.8 %reduce-scatter.2.cloned.1.call-start = ((), (), s32[]{:S(2)}) async-start(), calls=%async_computation.4 | async-start | bytes 2113536 | tf_op jit(solution)/shard_map/reduce_scatter | solution.py:26
Sparse Core Ops, SparseCore 0:
  11.8 247.8 all-gather.1
  269.6 51.7 all-reduce.1
  325.4 731.8 reduce-scatter.1
